TPU v7x, 32 devices: a whole 2x2x4 slice. The times are simulated.
32 devices in a mesh: tensor: 4 (over z), group: 4 (over y, core), cross: 2 (over x).
Axes of the slice: x: 2, y: 2, z: 4, core: 2. Of those that a mesh axis runs over, the one named last changes fastest.
Arguments:
- inputs: bfloat16 [16, 1568, 1024], P(('group', 'cross'), 'tensor'), may hold values from -6 to 6
- clips_here: int32 [8], P(('group', 'cross')), may hold values from 1 to 2, as said below
- first_gain: bfloat16 [1024], replicated, may hold values from 0.5 to 1.5
- first_shift: bfloat16 [1024], replicated, may hold values from -1.25 to 1.25
- query_key_value: bfloat16 [3, 1024, 1024], P(None, 'group', 'tensor'), may hold values from -0.1875 to 0.1875
- query_bias: bfloat16 [1024], P('tensor'), may hold values from -3 to 3
- value_bias: bfloat16 [1024], P('tensor'), may hold values from -0.1875 to 0.1875
- output_weight: bfloat16 [1024, 1024], P('tensor', 'group'), may hold values from -6 to 6
- output_bias: bfloat16 [1024], replicated, may hold values from -3 to 3
- second_gain: bfloat16 [1024], replicated, may hold values from 0.5 to 1.5
- second_shift: bfloat16 [1024], replicated, may hold values from -1.25 to 1.25
- expand_weight: bfloat16 [1024, 4096], P('group', 'tensor'), may hold values from -0.1875 to 0.1875
- expand_bias: bfloat16 [4096], P('tensor'), may hold values from -3 to 3
- contract_weight: bfloat16 [4096, 1024], P('tensor', 'group'), may hold values from -0.09375 to 0.09375
- contract_bias: bfloat16 [1024], replicated, may hold values from -3 to 3
- output_grad: bfloat16 [16, 1568, 1024], P(('group', 'cross'), 'tensor'), may hold values from -6 to 6
Outputs:
- output: bfloat16 [16, 1568, 1024], P(('group', 'cross'), 'tensor')
- input_grad: bfloat16 [16, 1568, 1024], P(('group', 'cross'), 'tensor')
- first_gain_grad: float32 [1024], P('group')
- first_shift_grad: float32 [1024], P('group')
- query_key_value_grad: float32 [3, 1024, 1024], P(None, 'group', 'tensor')
- query_bias_grad: float32 [1024], P(('tensor', 'group'))
- value_bias_grad: float32 [1024], P(('tensor', 'group'))
- output_weight_grad: float32 [1024, 1024], P('tensor', 'group')
- output_bias_grad: float32 [1024], P('group')
- second_gain_grad: float32 [1024], P('group')
- second_shift_grad: float32 [1024], P('group')
- expand_weight_grad: float32 [1024, 4096], P('group', 'tensor')
- expand_bias_grad: float32 [4096], P(('tensor', 'group'))
- contract_weight_grad: float32 [4096, 1024], P('tensor', 'group')
- contract_bias_grad: float32 [1024], P('group')
Inputs may be any that keep to these rules, and one draw needn't show every extreme that they name: Exactly half of the 8 data positions hold 2 clips and the others 1; slot p * 2 + j holds a clip if j < clips_here[p].
All inputs are finite; a program needn't handle non-finite values.
Results may differ from a plain program's by a relative error of at most 0.02.
Values may be sent and summed in bfloat16 or wider, within the bound.
A program may use at most 192 MiB of HBM per device.

v0:
```python
import jax
import jax.numpy as jnp
from jax import lax
from jax.sharding import PartitionSpec as P

HEAD = 64
epsilon = 1e-06
root_half = 0.7071067811865476
inv_root_two_pi = 0.3989422804014327


def normalize(values):
    center = values - jnp.mean(values, axis=-1, keepdims=True)
    inverse = lax.rsqrt(jnp.mean(center * center, axis=-1, keepdims=True) + epsilon)
    return (center * inverse, inverse)


def normalize_back(upstream, normed, inverse, norm_gain):
    scaled = upstream * norm_gain
    return inverse * (
        scaled
        - jnp.mean(scaled, axis=-1, keepdims=True)
        - normed * jnp.mean(scaled * normed, axis=-1, keepdims=True)
    )


def attend_forward(triple):
    query_rows, key_rows, value_rows = triple
    length = query_rows.shape[0]
    head_count = query_rows.shape[1] // HEAD
    key_heads = key_rows.reshape(length, head_count, HEAD)
    value_heads = value_rows.reshape(length, head_count, HEAD)
    query_parts = query_rows.reshape(2, length // 2, head_count, HEAD)

    def one_part(query_part):
        logits = jnp.einsum(
            "bhe,lhe->hbl", query_part, key_heads, preferred_element_type=jnp.float32
        ) * HEAD ** (-0.5)
        largest = jnp.max(logits, axis=-1, keepdims=True)
        powers = jnp.exp(logits - largest)
        totals = jnp.sum(powers, axis=-1, keepdims=True)
        probs = (powers / totals).astype(jnp.bfloat16)
        attention_result = jnp.einsum(
            "hbl,lhe->bhe", probs, value_heads, preferred_element_type=jnp.float32
        )
        return (attention_result.astype(jnp.bfloat16), largest + jnp.log(totals))

    attention_result, log_totals = lax.map(one_part, query_parts)
    return (attention_result.reshape(length, head_count * HEAD), log_totals)


def attend_backward(entries):
    query_rows, key_rows, value_rows, upstream_rows, log_totals = entries
    length = query_rows.shape[0]
    head_count = query_rows.shape[1] // HEAD
    key_heads = key_rows.reshape(length, head_count, HEAD)
    value_heads = value_rows.reshape(length, head_count, HEAD)
    query_parts = query_rows.reshape(2, length // 2, head_count, HEAD)
    upstream_parts = upstream_rows.reshape(2, length // 2, head_count, HEAD)

    def one_part(carry, part_items):
        key_grad, value_grad = carry
        query_part, upstream_part, log_total = part_items
        logits = jnp.einsum(
            "bhe,lhe->hbl", query_part, key_heads, preferred_element_type=jnp.float32
        ) * HEAD ** (-0.5)
        probs = jnp.exp(logits - log_total)
        prob_grad = jnp.einsum(
            "bhe,lhe->hbl", upstream_part, value_heads, preferred_element_type=jnp.float32
        )
        inner = jnp.sum(probs * prob_grad, axis=-1, keepdims=True)
        logit_grad = (probs * (prob_grad - inner) * HEAD ** (-0.5)).astype(jnp.bfloat16)
        query_grad = jnp.einsum(
            "hbl,lhe->bhe", logit_grad, key_heads, preferred_element_type=jnp.float32
        )
        key_grad = key_grad + jnp.einsum(
            "hbl,bhe->lhe", logit_grad, query_part, preferred_element_type=jnp.float32
        )
        value_grad = value_grad + jnp.einsum(
            "hbl,bhe->lhe",
            probs.astype(jnp.bfloat16),
            upstream_part,
            preferred_element_type=jnp.float32,
        )
        return ((key_grad, value_grad), query_grad.astype(jnp.bfloat16))

    empty_grad = jnp.zeros((length, head_count, HEAD), jnp.float32)
    (key_grad, value_grad), query_grads = lax.scan(
        one_part, (empty_grad, empty_grad), (query_parts, upstream_parts, log_totals)
    )
    width = head_count * HEAD
    return (
        query_grads.reshape(length, width),
        key_grad.astype(jnp.bfloat16).reshape(length, width),
        value_grad.astype(jnp.bfloat16).reshape(length, width),
    )


def gelu_slope(hidden_pre):
    normal_cdf = 0.5 * (1.0 + lax.erf(hidden_pre * root_half))
    normal_pdf = inv_root_two_pi * jnp.exp(-0.5 * hidden_pre * hidden_pre)
    return normal_cdf + hidden_pre * normal_pdf


def local(
    inputs,
    clips_here,
    first_gain,
    first_shift,
    query_key_value,
    query_bias,
    value_bias,
    output_weight,
    output_bias,
    second_gain,
    second_shift,
    expand_weight,
    expand_bias,
    contract_weight,
    contract_bias,
    output_grad,
):
    floating_kind = jnp.float32
    slot_count = inputs.shape[0]
    tensor_index = lax.axis_index("tensor")
    tensor_count = lax.axis_size("tensor")
    group_index = lax.axis_index("group")
    group_count = lax.axis_size("group")

    def widen(local_vector):
        width = local_vector.shape[0]
        return lax.dynamic_update_slice(
            jnp.zeros((width * tensor_count,), floating_kind), local_vector, (tensor_index * width,)
        )

    alive_mask = (jnp.arange(slot_count, dtype=jnp.int32) < clips_here[0]).astype(floating_kind)[
        :, None, None
    ]
    (
        triple_weight_complete,
        output_weight_complete,
        expand_weight_complete,
        contract_weight_complete,
    ) = (
        lax.all_gather(query_key_value, "group", axis=1, tiled=True),
        lax.all_gather(output_weight, "group", axis=1, tiled=True),
        lax.all_gather(expand_weight, "group", axis=0, tiled=True),
        lax.all_gather(contract_weight, "group", axis=1, tiled=True),
    )
    gain_one = first_gain.astype(floating_kind)
    gain_two = second_gain.astype(floating_kind)
    tokens = inputs.astype(floating_kind)
    first_plain, first_inverse = normalize(tokens)
    first_rows = (first_plain * gain_one + first_shift.astype(floating_kind)).astype(jnp.bfloat16)
    first_gathered = lax.all_gather(first_rows, "tensor", axis=1, tiled=True)
    bias_stack = jnp.stack([query_bias, jnp.zeros_like(query_bias), value_bias]).astype(
        floating_kind
    )
    projected = jnp.einsum(
        "ruh,nhm->nrum",
        first_gathered,
        triple_weight_complete,
        preferred_element_type=floating_kind,
    )
    projected = (projected + bias_stack[:, None, None, :]).astype(jnp.bfloat16)
    attention_result, log_totals = lax.map(
        attend_forward, (projected[0], projected[1], projected[2])
    )
    attention_terms = jnp.einsum(
        "hpx,xj->hpj",
        attention_result,
        output_weight_complete,
        preferred_element_type=floating_kind,
    )
    attention_part = lax.psum_scatter(
        attention_terms.astype(jnp.bfloat16), "tensor", scatter_dimension=1, tiled=True
    ).astype(jnp.float32)
    middle = tokens + attention_part + output_bias.astype(floating_kind)
    second_plain, second_inverse = normalize(middle)
    second_rows = (second_plain * gain_two + second_shift.astype(floating_kind)).astype(
        jnp.bfloat16
    )
    top_grad = output_grad.astype(floating_kind) * alive_mask
    feed_grad = top_grad.astype(jnp.bfloat16)
    contract_bias_part = jnp.sum(feed_grad.astype(floating_kind), axis=(0, 1))
    second_gathered = lax.all_gather(second_rows, "tensor", axis=1, tiled=True)
    hidden_pre = jnp.einsum(
        "njz,zc->njc", second_gathered, expand_weight_complete, preferred_element_type=floating_kind
    )
    hidden_pre = hidden_pre + expand_bias.astype(floating_kind)
    hidden_activation = jax.nn.gelu(hidden_pre, approximate=False).astype(jnp.bfloat16)
    feed_forward_terms = jnp.einsum(
        "ybj,jx->ybx",
        hidden_activation,
        contract_weight_complete,
        preferred_element_type=floating_kind,
    )
    feed_part = lax.psum_scatter(
        feed_forward_terms.astype(jnp.bfloat16), "tensor", scatter_dimension=1, tiled=True
    ).astype(jnp.float32)
    output = (middle + feed_part + contract_bias.astype(floating_kind)).astype(jnp.bfloat16)
    feed_grad_gathered = lax.all_gather(feed_grad, "tensor", axis=1, tiled=True)
    contract_weight_part = jnp.einsum(
        "gct,gcu->tu", hidden_activation, feed_grad_gathered, preferred_element_type=floating_kind
    )
    hidden_grad = jnp.einsum(
        "bxn,qn->bxq",
        feed_grad_gathered,
        contract_weight_complete,
        preferred_element_type=floating_kind,
    )
    preactivation_grad = (hidden_grad * gelu_slope(hidden_pre)).astype(jnp.bfloat16)
    expand_bias_vector = widen(jnp.sum(preactivation_grad.astype(floating_kind), axis=(0, 1)))
    expand_weight_part = jnp.einsum(
        "aew,aex->wx", second_gathered, preactivation_grad, preferred_element_type=floating_kind
    )
    second_terms = jnp.einsum(
        "rci,ei->rce",
        preactivation_grad,
        expand_weight_complete,
        preferred_element_type=floating_kind,
    )
    second_grad = lax.psum_scatter(
        second_terms.astype(jnp.bfloat16), "tensor", scatter_dimension=1, tiled=True
    ).astype(jnp.float32)
    second_gain_part = jnp.sum(second_grad * second_plain, axis=(0, 1))
    second_shift_part = jnp.sum(second_grad, axis=(0, 1))
    middle_grad = top_grad + normalize_back(second_grad, second_plain, second_inverse, gain_two)
    branch_grad = middle_grad.astype(jnp.bfloat16)
    output_bias_part = jnp.sum(branch_grad.astype(floating_kind), axis=(0, 1))
    branch_gathered = lax.all_gather(branch_grad, "tensor", axis=1, tiled=True)
    output_weight_part = jnp.einsum(
        "vat,vah->th", attention_result, branch_gathered, preferred_element_type=floating_kind
    )
    attended_grad = jnp.einsum(
        "ghv,cv->ghc", branch_gathered, output_weight_complete, preferred_element_type=floating_kind
    ).astype(jnp.bfloat16)
    query_grad, key_grad, value_grad = lax.map(
        attend_backward, (projected[0], projected[1], projected[2], attended_grad, log_totals)
    )
    triple_weight_gradient = jnp.stack([query_grad, key_grad, value_grad])
    query_bias_part = jnp.sum(query_grad.astype(floating_kind), axis=(0, 1))
    value_bias_part = jnp.sum(value_grad.astype(floating_kind), axis=(0, 1))
    triple_weight_part = jnp.einsum(
        "ayn,iayf->inf",
        first_gathered,
        triple_weight_gradient,
        preferred_element_type=floating_kind,
    )
    first_terms = jnp.einsum(
        "hpxw,hgw->pxg",
        triple_weight_gradient,
        triple_weight_complete,
        preferred_element_type=floating_kind,
    )
    first_grad = lax.psum_scatter(
        first_terms.astype(jnp.bfloat16), "tensor", scatter_dimension=1, tiled=True
    ).astype(jnp.float32)
    first_gain_part = jnp.sum(first_grad * first_plain, axis=(0, 1))
    first_shift_part = jnp.sum(first_grad, axis=(0, 1))
    input_grad = (
        middle_grad + normalize_back(first_grad, first_plain, first_inverse, gain_one)
    ).astype(jnp.bfloat16)
    large_parts = (triple_weight_part, output_weight_part, expand_weight_part, contract_weight_part)
    group_parts = (
        lax.psum_scatter(
            large_parts[0].astype(jnp.bfloat16), "group", scatter_dimension=1, tiled=True
        ).astype(jnp.float32),
        lax.psum_scatter(
            large_parts[1].astype(jnp.bfloat16), "group", scatter_dimension=1, tiled=True
        ).astype(jnp.float32),
        lax.psum_scatter(
            large_parts[2].astype(jnp.bfloat16), "group", scatter_dimension=0, tiled=True
        ).astype(jnp.float32),
        lax.psum_scatter(
            large_parts[3].astype(jnp.bfloat16), "group", scatter_dimension=1, tiled=True
        ).astype(jnp.float32),
    )
    large_sums = (
        lax.psum(group_parts[0].astype(jnp.bfloat16), "cross").astype(jnp.float32),
        lax.psum(group_parts[1].astype(jnp.bfloat16), "cross").astype(jnp.float32),
        lax.psum(group_parts[2].astype(jnp.bfloat16), "cross").astype(jnp.float32),
        lax.psum(group_parts[3].astype(jnp.bfloat16), "cross").astype(jnp.float32),
    )
    small_sums = lax.psum(
        (
            first_gain_part,
            first_shift_part,
            widen(query_bias_part),
            widen(value_bias_part),
            output_bias_part,
            second_gain_part,
            second_shift_part,
            expand_bias_vector,
            contract_bias_part,
        ),
        ("tensor", "group", "cross"),
    )

    def own_group(full_vector):
        width = full_vector.shape[0] // group_count
        return lax.dynamic_slice_in_dim(full_vector, group_index * width, width)

    def own_split(full_vector):
        width = full_vector.shape[0] // (group_count * tensor_count)
        return lax.dynamic_slice_in_dim(
            full_vector, (tensor_index * group_count + group_index) * width, width
        )

    return (
        output,
        input_grad,
        own_group(small_sums[0]),
        own_group(small_sums[1]),
        large_sums[0],
        own_split(small_sums[2]),
        own_split(small_sums[3]),
        large_sums[1],
        own_group(small_sums[4]),
        own_group(small_sums[5]),
        own_group(small_sums[6]),
        large_sums[2],
        own_split(small_sums[7]),
        large_sums[3],
        own_group(small_sums[8]),
    )


def solution(mesh):
    in_specs = (
        P(("group", "cross"), "tensor", None),
        P(("group", "cross")),
        P(),
        P(),
        P(None, "group", "tensor"),
        P("tensor"),
        P("tensor"),
        P("tensor", "group"),
        P(),
        P(),
        P(),
        P("group", "tensor"),
        P("tensor"),
        P("tensor", "group"),
        P(),
        P(("group", "cross"), "tensor", None),
    )
    out_specs = (
        P(("group", "cross"), "tensor", None),
        P(("group", "cross"), "tensor", None),
        P("group"),
        P("group"),
        P(None, "group", "tensor"),
        P(("tensor", "group")),
        P(("tensor", "group")),
        P("tensor", "group"),
        P("group"),
        P("group"),
        P("group"),
        P("group", "tensor"),
        P(("tensor", "group")),
        P("tensor", "group"),
        P("group"),
    )
    return jax.shard_map(local, mesh=mesh, in_specs=in_specs, out_specs=out_specs, check_vma=False)
```

profile of v0, /device:TPU:0, one launch (start us, length us, event | category | flops | bytes accessed | tf_op | source)
XLA Modules:
  0.0 1773.0 jit_solution(4338053443137835705)
XLA Ops:
  15.8 10.8 all_gather.26
  26.7 6.8 all-gather.10.cloned.1.call-done
  33.5 120.5 %all-gather.8.cloned.1.call-done = bf16[2,1568,1024]{2,1,0:T(8,128)(2,1)} async-done(((bf16[2,392,1024]{2,1,0:T(8,128)(2,1)}), bf16[2,1568,1024]{2,1,0:T(8,128)(2,1)}) %all-gather.8.cloned.1.call-update) | async-done | bytes 6422544 | tf_op jit(solution)/shard_map/all_gather | solution.py:155
  154.0 7.8 fusion.79
  173.9 81.3 %while.54 = (s32[]{:T(128)}, bf16[2,1568,256]{1,2,0:T(8,128)(2,1)}, f32[2,2,4,784,1]{3,2,1,4,0:T(4,128)}, bf16[2,1568,256]{1,2,0:T(8,128)(2,1)}, bf16[2,1568,256...) while((s32[]{:T(128)}, bf16[2,1568,256]{1,2,0:T(8,128)(2,1)}, ...), condition=%wide.region_7.8_spmd, body=%wide.region_2.7_spmd.sunk | while | flops 1303268352 | bytes 87527496 | solution.py:166
  180.3 30.0 %while.57 = (s32[]{:T(128)}, bf16[2,784,4,64]{1,3,2,0:T(8,128)(2,1)}, f32[2,4,784,1]{2,1,3,0:T(4,128)S(1)}, bf16[2,784,4,64]{1,3,2,0:T(8,128)(2,1)}, bf16[1568,4...) while((s32[]{:T(128)}, bf16[2,784,4,64]{1,3,2,0:T(8,128)(2,1)}, ...), condition=%wide.region_6.6_spmd, body=%wide.region_3.5_spmd.sunk | while | flops 1303268352 | bytes 61734240 | solution.py:48
  188.7 6.5 fusion.183
  203.7 6.5 fusion.183
  220.9 30.0 %while.57 = (s32[]{:T(128)}, bf16[2,784,4,64]{1,3,2,0:T(8,128)(2,1)}, f32[2,4,784,1]{2,1,3,0:T(4,128)S(1)}, bf16[2,784,4,64]{1,3,2,0:T(8,128)(2,1)}, bf16[1568,4...) while((s32[]{:T(128)}, bf16[2,784,4,64]{1,3,2,0:T(8,128)(2,1)}, ...), condition=%wide.region_6.6_spmd, body=%wide.region_3.5_spmd.sunk | while | flops 1303268352 | bytes 61734240 | solution.py:48
  229.3 6.5 fusion.183
  244.3 6.5 fusion.183
  259.2 13.9 copy.84
  273.2 5.4 copy.97
  279.3 110.5 %reduce-scatter.25.cloned.1.call-done = bf16[392,2048]{1,0:T(8,128)(2,1)} async-done(((bf16[1568,2048]{1,0:T(8,128)(2,1)}), bf16[392,2048]{1,0:T(8,128)(2,1)}) %reduce-scatter.25.cloned.1.call-update) | async-done | bytes 1605648
  403.3 11.0 all-gather.14.cloned.1.call-done
  414.4 119.5 %all-gather.12.cloned.1.call-done = bf16[2,1568,1024]{2,1,0:T(8,128)(2,1)} async-done(((bf16[2,392,1024]{2,1,0:T(8,128)(2,1)}), bf16[2,1568,1024]{2,1,0:T(8,128)(2,1)}) %all-gather.12.cloned.1.call-update) | async-done | bytes 6422544 | tf_op jit(solution)/shard_map/all_gather | solution.py:186
  533.9 19.7 %fusion.109 = (u8[1568,1024]{1,0:T(8,128)(4,1)}, u8[1568,1024]{1,0:T(8,128)(4,1)}, f32[2,1568,1024]{2,1,0:T(8,128)}) fusion(f32[1024]{0:T(1024)S(1)} %convert_element_type.188, bf16[2,1568,1024]{2,1,0:T(8,128)(2,1)} %all-gather.12.cloned.1.call-done, bf16[1024,1024]{1,0:T(8,128)(2,1)} %all-gather.14.cloned.1.call-done), kind=kOutput, calls=%fused_computation.148 | convolution fusion | flops 6618415104 | bytes 24580096 | tf_op jit(solution)/shard_map/njz,zc->njc/dot_general | solution.py:187
  556.4 119.1 %all-gather.18.cloned.1.call-done = bf16[2,1568,1024]{2,1,0:T(8,128)(2,1)} async-done(((bf16[2,392,1024]{2,1,0:T(8,128)(2,1)}), bf16[2,1568,1024]{2,1,0:T(8,128)(2,1)}) %all-gather.18.cloned.1.call-update) | async-done | bytes 6422544 | tf_op jit(solution)/shard_map/all_gather | solution.py:202
  675.5 15.1 convert_reduce_fusion
  690.6 7.5 convolution_convert_fusion
  698.1 13.7 copy.88
  711.8 5.4 copy.99
  717.3 111.1 %reduce-scatter.29.cloned.1.call-done = bf16[392,2048]{1,0:T(8,128)(2,1)} async-done(((bf16[1568,2048]{1,0:T(8,128)(2,1)}), bf16[392,2048]{1,0:T(8,128)(2,1)}) %reduce-scatter.29.cloned.1.call-update) | async-done | bytes 1605648
  828.5 5.3 reshape.178
  841.8 12.7 bitcast_convert_fusion.2
  854.6 31.3 %fusion.62 = bf16[2,1568,1024]{2,1,0:T(8,128)(2,1)S(1)} fusion(f32[2,1568,1024]{2,1,0:T(8,128)} %get-tuple-element.432, f32[1024]{0:T(1024)S(1)} %convert_element_type.188, u8[1568,1024]{1,0:T(8,128)(4,1)S(1)} %copy-done.29, u8[1568,1024]{1,0:T(8,128)(4,1)S(1)} %copy-done.28), kind=kLoop, calls=%fused_computation.65 | loop fusion | flops 227999744 | bytes 22482944 | tf_op jit(solution)/shard_map/convert_element_type | solution.py:191
  888.6 10.5 bitcast_convert_fusion.1
  899.2 60.8 %all-gather.20.cloned.1.call-done = bf16[2,1568,1024]{2,1,0:T(8,128)(2,1)} async-done(((bf16[2,392,1024]{2,1,0:T(8,128)(2,1)}), bf16[2,1568,1024]{2,1,0:T(8,128)(2,1)}) %all-gather.20.cloned.1.call-update) | async-done | bytes 6422544 | tf_op jit(solution)/shard_map/all_gather | solution.py:231
  967.3 388.1 %while.56 = (s32[]{:T(128)}, bf16[2,1568,256]{1,2,0:T(8,128)(2,1)}, bf16[2,1568,256]{2,1,0:T(8,128)(2,1)}, bf16[2,1568,256]{1,2,0:T(8,128)(2,1)}, bf16[2,1568,25...) while((s32[]{:T(128)}, bf16[2,1568,256]{1,2,0:T(8,128)(2,1)}, ...), condition=%wide.region_19.20_spmd, body=%wide.region_15.19_spmd.sunk | while | flops 3213581312 | bytes 417577472 | solution.py:238
  977.7 174.2 %while.58 = (s32[]{:T(128)}, f32[1568,4,64]{0,2,1:T(8,128)}, f32[1568,4,64]{0,2,1:T(8,128)}, bf16[2,784,4,64]{1,3,2,0:T(8,128)(2,1)}, bf16[2,784,4,64]{1,3,2,0:T...) while((s32[]{:T(128)}, f32[1568,4,64]{0,2,1:T(8,128)}, ...), condition=%wide.region_18.18_spmd.clone, body=%wide.region_16.17_spmd.clone.sunk | while | flops 3212778496 | bytes 332231680 | solution.py:88
  977.7 5.1 subtract_exponential_fusion.3
  982.9 5.3 fusion.178
  990.5 11.9 fusion.176
  1002.5 31.2 %fusion.179 = bf16[2,784,4,64]{1,3,2,0:T(8,128)(2,1)} fusion(bf16[2,784,4,64]{1,3,2,0:T(8,128)(2,1)} %get-tuple-element.710, s32[]{:T(128)S(6)} %copy.167, bf16[1568,4,64]{0,2,1:T(8,128)(2,1)} %get-tuple-element.723, f32[4,784,1568]{2,1,0:T(8,128)} %copy-done, f32[4,784,1568]{2,1,0:T(8,128)} %fusion.176), kind=kOutput, calls=%fused_computation.34.clone.1 | convolution fusion | flops 654199424 | bytes 84803584 | tf_op jit(solution)/shard_map/while/body/eval_jaxpr/while/body/eval_jaxpr/hbl,lhe->bhe/dot_general | solution.py:73
  1033.7 30.1 %fusion.177 = f32[1568,4,64]{0,2,1:T(8,128)S(1)} fusion(f32[4,784,1568]{2,1,0:T(8,128)} %copy-done, f32[4,784,1568]{2,1,0:T(8,128)} %fusion.176, f32[1568,4,64]{0,2,1:T(8,128)S(1)} %copy-done.13, pred[]{:T(512)S(6)} %compare.3, bf16[2,784,4,64]{1,3,2,0:T(8,128)(2,1)S(1)} %copy-done.2, s32[]{:T(128)S(6)} %copy.167), kind=kOutput, calls=%fused_computation.30.clone.1 | convolution fusion | flops 654801536 | bytes 87261192 | tf_op jit(solution)/shard_map/while/body/eval_jaxpr/while/body/eval_jaxpr/hbl,bhe->lhe/dot_general | solution.py:76
  1070.1 7.2 fusion.178
  1078.3 11.2 fusion.176
  1089.4 31.2 %fusion.179 = bf16[2,784,4,64]{1,3,2,0:T(8,128)(2,1)} fusion(bf16[2,784,4,64]{1,3,2,0:T(8,128)(2,1)} %get-tuple-element.710, s32[]{:T(128)S(6)} %copy.167, bf16[1568,4,64]{0,2,1:T(8,128)(2,1)} %get-tuple-element.723, f32[4,784,1568]{2,1,0:T(8,128)} %copy-done, f32[4,784,1568]{2,1,0:T(8,128)} %fusion.176), kind=kOutput, calls=%fused_computation.34.clone.1 | convolution fusion | flops 654199424 | bytes 84803584 | tf_op jit(solution)/shard_map/while/body/eval_jaxpr/while/body/eval_jaxpr/hbl,lhe->bhe/dot_general | solution.py:73
  1120.6 30.1 %fusion.177 = f32[1568,4,64]{0,2,1:T(8,128)S(1)} fusion(f32[4,784,1568]{2,1,0:T(8,128)} %copy-done, f32[4,784,1568]{2,1,0:T(8,128)} %fusion.176, f32[1568,4,64]{0,2,1:T(8,128)S(1)} %copy-done.13, pred[]{:T(512)S(6)} %compare.3, bf16[2,784,4,64]{1,3,2,0:T(8,128)(2,1)S(1)} %copy-done.2, s32[]{:T(128)S(6)} %copy.167), kind=kOutput, calls=%fused_computation.30.clone.1 | convolution fusion | flops 654801536 | bytes 87261192 | tf_op jit(solution)/shard_map/while/body/eval_jaxpr/while/body/eval_jaxpr/hbl,bhe->lhe/dot_general | solution.py:76
  1171.9 173.4 %while.58 = (s32[]{:T(128)}, f32[1568,4,64]{0,2,1:T(8,128)}, f32[1568,4,64]{0,2,1:T(8,128)}, bf16[2,784,4,64]{1,3,2,0:T(8,128)(2,1)}, bf16[2,784,4,64]{1,3,2,0:T...) while((s32[]{:T(128)}, f32[1568,4,64]{0,2,1:T(8,128)}, ...), condition=%wide.region_18.18_spmd.clone, body=%wide.region_16.17_spmd.clone.sunk | while | flops 3212778496 | bytes 332231680 | solution.py:88
  1177.0 5.2 fusion.178
  1184.6 11.2 fusion.176
  1195.8 31.2 %fusion.179 = bf16[2,784,4,64]{1,3,2,0:T(8,128)(2,1)} fusion(bf16[2,784,4,64]{1,3,2,0:T(8,128)(2,1)} %get-tuple-element.710, s32[]{:T(128)S(6)} %copy.167, bf16[1568,4,64]{0,2,1:T(8,128)(2,1)} %get-tuple-element.723, f32[4,784,1568]{2,1,0:T(8,128)} %copy-done, f32[4,784,1568]{2,1,0:T(8,128)} %fusion.176), kind=kOutput, calls=%fused_computation.34.clone.1 | convolution fusion | flops 654199424 | bytes 84803584 | tf_op jit(solution)/shard_map/while/body/eval_jaxpr/while/body/eval_jaxpr/hbl,lhe->bhe/dot_general | solution.py:73
  1227.0 30.1 %fusion.177 = f32[1568,4,64]{0,2,1:T(8,128)S(1)} fusion(f32[4,784,1568]{2,1,0:T(8,128)} %copy-done, f32[4,784,1568]{2,1,0:T(8,128)} %fusion.176, f32[1568,4,64]{0,2,1:T(8,128)S(1)} %copy-done.13, pred[]{:T(512)S(6)} %compare.3, bf16[2,784,4,64]{1,3,2,0:T(8,128)(2,1)S(1)} %copy-done.2, s32[]{:T(128)S(6)} %copy.167), kind=kOutput, calls=%fused_computation.30.clone.1 | convolution fusion | flops 654801536 | bytes 87261192 | tf_op jit(solution)/shard_map/while/body/eval_jaxpr/while/body/eval_jaxpr/hbl,bhe->lhe/dot_general | solution.py:76
  1263.4 7.2 fusion.178
  1271.6 11.2 fusion.176
  1282.8 31.2 %fusion.179 = bf16[2,784,4,64]{1,3,2,0:T(8,128)(2,1)} fusion(bf16[2,784,4,64]{1,3,2,0:T(8,128)(2,1)} %get-tuple-element.710, s32[]{:T(128)S(6)} %copy.167, bf16[1568,4,64]{0,2,1:T(8,128)(2,1)} %get-tuple-element.723, f32[4,784,1568]{2,1,0:T(8,128)} %copy-done, f32[4,784,1568]{2,1,0:T(8,128)} %fusion.176), kind=kOutput, calls=%fused_computation.34.clone.1 | convolution fusion | flops 654199424 | bytes 84803584 | tf_op jit(solution)/shard_map/while/body/eval_jaxpr/while/body/eval_jaxpr/hbl,lhe->bhe/dot_general | solution.py:73
  1314.0 30.1 %fusion.177 = f32[1568,4,64]{0,2,1:T(8,128)S(1)} fusion(f32[4,784,1568]{2,1,0:T(8,128)} %copy-done, f32[4,784,1568]{2,1,0:T(8,128)} %fusion.176, f32[1568,4,64]{0,2,1:T(8,128)S(1)} %copy-done.13, pred[]{:T(512)S(6)} %compare.3, bf16[2,784,4,64]{1,3,2,0:T(8,128)(2,1)S(1)} %copy-done.2, s32[]{:T(128)S(6)} %copy.167), kind=kOutput, calls=%fused_computation.30.clone.1 | convolution fusion | flops 654801536 | bytes 87261192 | tf_op jit(solution)/shard_map/while/body/eval_jaxpr/while/body/eval_jaxpr/hbl,bhe->lhe/dot_general | solution.py:76
  1361.4 5.5 fusion.122
  1367.0 10.2 fusion.119
  1377.2 10.2 convolution_convert_fusion.1
  1387.5 13.7 copy.86
  1401.2 5.4 copy.98
  1406.8 11.1 reduce-scatter.17.cloned.1.call-done
  1417.9 7.6 bitcast_convert_fusion
  1425.5 13.7 copy.90
  1439.2 5.4 copy.100
  1445.6 87.3 %reduce-scatter.27.cloned.1.call-done = bf16[392,2048]{1,0:T(8,128)(2,1)} async-done(((bf16[1568,2048]{1,0:T(8,128)(2,1)}), bf16[392,2048]{1,0:T(8,128)(2,1)}) %reduce-scatter.27.cloned.1.call-update) | async-done | bytes 1605648
  1532.9 5.3 reshape.176
  1539.4 48.4 %all-reduce.4.cloned.1.call-done = (bf16[3,256,256]{1,2,0:T(8,128)(2,1)}, bf16[256,256]{1,0:T(8,128)(2,1)}, bf16[256,1024]{1,0:T(8,128)(2,1)}, bf16[1024,256]{1,0:T(8,128)(2,1)}) async-done(((bf16[3,256,256]{1,2,0:T(8,128)(2,1)}, bf16[256,256]{1,0:T(8,128)(2,1)}, bf16[256,1024]{1,0:T(8,128)(2,1)}, bf16[1024,256]{1,0:T(8,128)(2,1)}), (bf16[3,256,256]{1,2,0:T(8,128)(2,1)}, bf16[256,256]{1,0:T(8,128)(2,1)}, ...) | async-done | bytes 1572880 | tf_op jit(solution)/shard_map/psum | solution.py:280
  1594.9 108.1 %reduce-scatter.31.cloned.1.call-done = bf16[392,2048]{1,0:T(8,128)(2,1)} async-done(((bf16[1568,2048]{1,0:T(8,128)(2,1)}), bf16[392,2048]{1,0:T(8,128)(2,1)}) %reduce-scatter.31.cloned.1.call-update) | async-done | bytes 1605648
  1703.0 5.3 reshape.180
  1711.6 41.9 %all-reduce = (f32[1024]{0:T(1024)S(1)}, f32[1024]{0:T(1024)S(1)}, f32[1024]{0:T(1024)S(1)}, f32[1024]{0:T(1024)S(1)}, f32[1024]{0:T(1024)S(1)}, /*index=5*/f32[...) all-reduce(f32[1024]{0:T(1024)S(1)} %get-tuple-element.338, ...), channel_id=1, replica_groups=mesh['tensor'=4,'group'=4,'cross'=2] {'tensor','group','cross'}, use_global_device_ids=true, to_apply=%region_24.25 | all-reduce | flops 12288 | bytes 98304 | tf_op jit(solution)/shard_map/psum | solution.py:285
  1759.1 7.1 fusion.97
  (357 shorter events, 204.5 us)
Async XLA Ops:
  7.2 6.6 copy-start.3
  7.2 26.3 %all-gather.10.cloned.1.call-start = ((), (), s32[]{:S(2)}) async-start(), calls=%async_computation.9 | async-start | bytes 1966080 | tf_op jit(solution)/shard_map/all_gather | solution.py:145
  7.9 146.1 %all-gather.8.cloned.1.call-start = ((), (), s32[]{:S(2)}) async-start(), calls=%async_computation.8 | async-start | bytes 8028160 | tf_op jit(solution)/shard_map/all_gather | solution.py:155
  15.6 374.2 %reduce-scatter.25.cloned.1.call-start = ((), (), s32[]{:S(2)}) async-start(), calls=%async_computation.19 | async-start | bytes 8028160
  174.0 6.3 copy-start.8
  214.6 6.2 copy-start.8
  278.6 115.7 %copy-start.4 = (bf16[2,392,1024]{2,1,0:T(8,128)(2,1)S(1)}, bf16[2,392,1024]{2,1,0:T(8,128)(2,1)}, u32[]{:S(2)}) copy-start(bf16[2,392,1024]{2,1,0:T(8,128)(2,1)} %param.24) | copy-start | bytes 4816900
  278.6 135.8 %all-gather.14.cloned.1.call-start = ((), (), s32[]{:S(2)}) async-start(), calls=%async_computation.11 | async-start | bytes 2621440 | tf_op jit(solution)/shard_map/all_gather | solution.py:147
  279.2 254.7 %all-gather.12.cloned.1.call-start = ((), (), s32[]{:S(2)}) async-start(), calls=%async_computation.10 | async-start | bytes 8028160 | tf_op jit(solution)/shard_map/all_gather | solution.py:186
  279.3 558.7 %copy-start.32 = (f32[1024]{0:T(1024)}, f32[1024]{0:T(1024)S(1)}, u32[]{:S(2)}) copy-start(f32[1024]{0:T(1024)S(1)} %convert_element_type.184) | copy-start | bytes 12292
  279.3 558.7 %copy-start.39 = (f32[1024]{0:T(1024)}, f32[1024]{0:T(1024)S(1)}, u32[]{:S(2)}) copy-start(f32[1024]{0:T(1024)S(1)} %convert_element_type.185) | copy-start | bytes 12292
  394.3 443.7 %copy-start.6 = (bf16[392,2,1024]{2,1,0:T(2,128)(2,1)}, bf16[392,2,1024]{2,1,0:T(2,128)(2,1)S(1)}, u32[]{:S(2)}) copy-start(bf16[392,2,1024]{2,1,0:T(2,128)(2,1)S(1)} %reshape.174) | copy-start | bytes 4816900
  394.9 443.1 %copy-start.34 = (f32[2,392]{1,0:T(2,128)}, f32[2,392]{1,0:T(2,128)S(1)}, u32[]{:S(2)}) copy-start(f32[2,392]{1,0:T(2,128)S(1)} %broadcast_multiply_fusion.4) | copy-start | bytes 9412
  395.8 442.2 %copy-start.41 = (f32[2,392]{1,0:T(2,128)}, f32[2,392]{1,0:T(2,128)S(1)}, u32[]{:S(2)}) copy-start(f32[2,392]{1,0:T(2,128)S(1)} %add_rsqrt_fusion) | copy-start | bytes 9412
  397.8 5.5 copy-start.61
  397.9 158.5 %all-gather.16.cloned.1.call-start = ((), (), s32[]{:S(2)}) async-start(), calls=%async_computation.12 | async-start | bytes 2621440 | tf_op jit(solution)/shard_map/all_gather | solution.py:148
  398.5 277.0 %all-gather.18.cloned.1.call-start = ((), (), s32[]{:S(2)}) async-start(), calls=%async_computation.13 | async-start | bytes 8028160 | tf_op jit(solution)/shard_map/all_gather | solution.py:202
  399.2 438.9 %copy-start.55 = (f32[2]{0:T(128)}, f32[2]{0:T(128)S(1)}, u32[]{:S(2)}) copy-start(f32[2]{0:T(128)S(1)} %compare_convert_fusion) | copy-start | bytes 28
  403.3 425.2 %reduce-scatter.29.cloned.1.call-start = ((), (), s32[]{:S(2)}) async-start(), calls=%async_computation.21 | async-start | bytes 8028160
  675.5 15.1 copy-start.63
  690.6 7.5 copy-start.66
  717.3 242.6 %all-gather.20.cloned.1.call-start = ((), (), s32[]{:S(2)}) async-start(), calls=%async_computation.14 | async-start | bytes 8028160 | tf_op jit(solution)/shard_map/all_gather | solution.py:231
  841.7 565.0 %reduce-scatter.21.cloned.1.call-start = ((), (), s32[]{:S(2)}) async-start(), calls=%async_computation.17 | async-start | bytes 2621440 | tf_op jit(solution)/shard_map/reduce_scatter | solution.py:272
  841.8 12.8 copy-start.28
  841.8 12.8 copy-start.29
  854.5 552.2 %reduce-scatter.23.cloned.1.call-start = ((), (), s32[]{:S(2)}) async-start(), calls=%async_computation.18 | async-start | bytes 2621440 | tf_op jit(solution)/shard_map/reduce_scatter | solution.py:275
  888.5 71.4 %copy-start.27 = (bf16[256,1024]{1,0:T(8,128)(2,1)S(1)}, bf16[256,1024]{1,0:T(8,128)(2,1)}, u32[]{:S(2)}) copy-start(bf16[256,1024]{1,0:T(8,128)(2,1)} %all_gather.26) | copy-start | bytes 1572868
  899.1 507.6 %reduce-scatter.19.cloned.1.call-start = ((), (), s32[]{:S(2)}) async-start(), calls=%async_computation.16 | async-start | bytes 655360 | tf_op jit(solution)/shard_map/reduce_scatter | solution.py:269
  982.9 7.7 copy-start
  1002.4 31.2 %copy-start.2 = (bf16[2,784,4,64]{1,3,2,0:T(8,128)(2,1)S(1)}, bf16[2,784,4,64]{1,3,2,0:T(8,128)(2,1)}, u32[]{:S(2)}) copy-start(bf16[2,784,4,64]{1,3,2,0:T(8,128)(2,1)} %get-tuple-element.722) | copy-start | bytes 2408452 | tf_op jit(solution)/shard_map/while/body/eval_jaxpr/while
  1002.5 31.2 %copy-start.13 = (f32[1568,4,64]{0,2,1:T(8,128)S(1)}, f32[1568,4,64]{0,2,1:T(8,128)}, u32[]{:S(2)}) copy-start(f32[1568,4,64]{0,2,1:T(8,128)} %get-tuple-element.708) | copy-start | bytes 4816900 | tf_op jit(solution)/shard_map/while/body/eval_jaxpr/while
  1070.1 8.2 copy-start
  1089.4 31.2 %copy-start.2 = (bf16[2,784,4,64]{1,3,2,0:T(8,128)(2,1)S(1)}, bf16[2,784,4,64]{1,3,2,0:T(8,128)(2,1)}, u32[]{:S(2)}) copy-start(bf16[2,784,4,64]{1,3,2,0:T(8,128)(2,1)} %get-tuple-element.722) | copy-start | bytes 2408452 | tf_op jit(solution)/shard_map/while/body/eval_jaxpr/while
  1089.4 31.2 %copy-start.13 = (f32[1568,4,64]{0,2,1:T(8,128)S(1)}, f32[1568,4,64]{0,2,1:T(8,128)}, u32[]{:S(2)}) copy-start(f32[1568,4,64]{0,2,1:T(8,128)} %get-tuple-element.708) | copy-start | bytes 4816900 | tf_op jit(solution)/shard_map/while/body/eval_jaxpr/while
  1177.0 7.6 copy-start
  1195.8 31.2 %copy-start.2 = (bf16[2,784,4,64]{1,3,2,0:T(8,128)(2,1)S(1)}, bf16[2,784,4,64]{1,3,2,0:T(8,128)(2,1)}, u32[]{:S(2)}) copy-start(bf16[2,784,4,64]{1,3,2,0:T(8,128)(2,1)} %get-tuple-element.722) | copy-start | bytes 2408452 | tf_op jit(solution)/shard_map/while/body/eval_jaxpr/while
  1195.8 31.2 %copy-start.13 = (f32[1568,4,64]{0,2,1:T(8,128)S(1)}, f32[1568,4,64]{0,2,1:T(8,128)}, u32[]{:S(2)}) copy-start(f32[1568,4,64]{0,2,1:T(8,128)} %get-tuple-element.708) | copy-start | bytes 4816900 | tf_op jit(solution)/shard_map/while/body/eval_jaxpr/while
  1263.4 8.2 copy-start
  1282.8 31.2 %copy-start.2 = (bf16[2,784,4,64]{1,3,2,0:T(8,128)(2,1)S(1)}, bf16[2,784,4,64]{1,3,2,0:T(8,128)(2,1)}, u32[]{:S(2)}) copy-start(bf16[2,784,4,64]{1,3,2,0:T(8,128)(2,1)} %get-tuple-element.722) | copy-start | bytes 2408452 | tf_op jit(solution)/shard_map/while/body/eval_jaxpr/while
  1282.8 31.2 %copy-start.13 = (f32[1568,4,64]{0,2,1:T(8,128)S(1)}, f32[1568,4,64]{0,2,1:T(8,128)}, u32[]{:S(2)}) copy-start(f32[1568,4,64]{0,2,1:T(8,128)} %get-tuple-element.708) | copy-start | bytes 4816900 | tf_op jit(solution)/shard_map/while/body/eval_jaxpr/while
  1355.4 6.0 copy-start.25
  1366.9 50.9 %reduce-scatter.17.cloned.1.call-start = ((), (), s32[]{:S(2)}) async-start(), calls=%async_computation.15 | async-start | bytes 1966080 | tf_op jit(solution)/shard_map/reduce_scatter | solution.py:266
  1377.2 155.7 %reduce-scatter.27.cloned.1.call-start = ((), (), s32[]{:S(2)}) async-start(), calls=%async_computation.20 | async-start | bytes 8028160
  1406.6 11.3 copy-start.30
  1406.6 181.2 %all-reduce.4.cloned.1.call-start = ((), (), s32[]{:S(2)}) async-start(), calls=%async_computation.23 | async-start | bytes 3145728 | tf_op jit(solution)/shard_map/psum | solution.py:280
  1417.9 285.2 %reduce-scatter.31.cloned.1.call-start = ((), (), s32[]{:S(2)}) async-start(), calls=%async_computation.22 | async-start | bytes 8028160
  1444.7 93.6 %copy-start.18 = (bf16[2,1568,256]{1,2,0:T(8,128)(2,1)S(1)}, bf16[2,1568,256]{1,2,0:T(8,128)(2,1)}, u32[]{:S(2)}) copy-start(bf16[2,1568,256]{1,2,0:T(8,128)(2,1)} %get-tuple-element.183) | copy-start | bytes 4816900
  1587.8 6.0 copy-start.31
  1591.5 116.8 %copy-start.5 = (bf16[2,392,1024]{2,1,0:T(8,128)(2,1)S(1)}, bf16[2,392,1024]{2,1,0:T(8,128)(2,1)}, u32[]{:S(2)}) copy-start(bf16[2,392,1024]{2,1,0:T(8,128)(2,1)} %param.24) | copy-start | bytes 4816900
  1591.5 116.8 %copy-start.38 = (f32[2,392]{1,0:T(2,128)S(1)}, f32[2,392]{1,0:T(2,128)}, u32[]{:S(2)}) copy-start(f32[2,392]{1,0:T(2,128)} %copy-done.37) | copy-start | bytes 9412
  1591.5 116.8 %copy-start.44 = (f32[1024]{0:T(1024)S(1)}, f32[1024]{0:T(1024)}, u32[]{:S(2)}) copy-start(f32[1024]{0:T(1024)} %copy-done.43) | copy-start | bytes 12292
  1591.5 116.8 %copy-start.46 = (f32[2,392]{1,0:T(2,128)S(1)}, f32[2,392]{1,0:T(2,128)}, u32[]{:S(2)}) copy-start(f32[2,392]{1,0:T(2,128)} %copy-done.45) | copy-start | bytes 9412
  1594.8 116.7 %copy-start.51 = (f32[1024]{0:T(1024)S(1)}, f32[1024]{0:T(1024)}, u32[]{:S(2)}) copy-start(f32[1024]{0:T(1024)} %get-tuple-element.417) | copy-start | bytes 12292
  1594.8 116.7 %copy-start.52 = (f32[1024]{0:T(1024)S(1)}, f32[1024]{0:T(1024)}, u32[]{:S(2)}) copy-start(f32[1024]{0:T(1024)} %get-tuple-element.336) | copy-start | bytes 12292
  1594.8 116.7 %copy-start.53 = (f32[1024]{0:T(1024)S(1)}, f32[1024]{0:T(1024)}, u32[]{:S(2)}) copy-start(f32[1024]{0:T(1024)} %get-tuple-element.342) | copy-start | bytes 12292
  1594.8 116.7 %copy-start.54 = (f32[1024]{0:T(1024)S(1)}, f32[1024]{0:T(1024)}, u32[]{:S(2)}) copy-start(f32[1024]{0:T(1024)} %get-tuple-element.419) | copy-start | bytes 12292
  1594.9 164.2 %copy-start.7 = (bf16[392,2,1024]{2,1,0:T(2,128)(2,1)S(1)}, bf16[392,2,1024]{2,1,0:T(2,128)(2,1)}, u32[]{:S(2)}) copy-start(bf16[392,2,1024]{2,1,0:T(2,128)(2,1)} %copy-done.6) | copy-start | bytes 4816900
  1594.9 164.2 %copy-start.33 = (f32[1024]{0:T(1024)S(1)}, f32[1024]{0:T(1024)}, u32[]{:S(2)}) copy-start(f32[1024]{0:T(1024)} %copy-done.32) | copy-start | bytes 12292
  1594.9 164.2 %copy-start.35 = (f32[2,392]{1,0:T(2,128)S(1)}, f32[2,392]{1,0:T(2,128)}, u32[]{:S(2)}) copy-start(f32[2,392]{1,0:T(2,128)} %copy-done.34) | copy-start | bytes 9412
  1594.9 164.2 %copy-start.40 = (f32[1024]{0:T(1024)S(1)}, f32[1024]{0:T(1024)}, u32[]{:S(2)}) copy-start(f32[1024]{0:T(1024)} %copy-done.39) | copy-start | bytes 12292
  1594.9 164.2 %copy-start.42 = (f32[2,392]{1,0:T(2,128)S(1)}, f32[2,392]{1,0:T(2,128)}, u32[]{:S(2)}) copy-start(f32[2,392]{1,0:T(2,128)} %copy-done.41) | copy-start | bytes 9412
  1594.9 164.2 %copy-start.48 = (f32[2,392]{1,0:T(2,128)S(1)}, f32[2,392]{1,0:T(2,128)}, u32[]{:S(2)}) copy-start(f32[2,392]{1,0:T(2,128)} %copy-done.47) | copy-start | bytes 9412
  1594.9 164.2 %copy-start.50 = (f32[2,392]{1,0:T(2,128)S(1)}, f32[2,392]{1,0:T(2,128)}, u32[]{:S(2)}) copy-start(f32[2,392]{1,0:T(2,128)} %copy-done.49) | copy-start | bytes 9412
  1594.9 164.2 %copy-start.56 = (f32[2]{0:T(128)S(1)}, f32[2]{0:T(128)}, u32[]{:S(2)}) copy-start(f32[2]{0:T(128)} %copy-done.55) | copy-start | bytes 28
  (42 other events, 113.0 us)
Sparse Core Ops, SparseCore 0:
  9.6 23.8 all-gather.9
  35.6 118.3 all-gather.7
  278.7 111.0 reduce-scatter.24
  391.2 23.0 all-gather.13
  416.4 117.4 all-gather.11
  535.3 21.0 all-gather.15
  557.9 117.4 all-gather.17
  717.4 111.0 reduce-scatter.28
  841.8 118.0 all-gather.19
  962.3 29.5 reduce-scatter.20
  994.6 31.4 reduce-scatter.22
  1367.1 19.8 reduce-scatter.18
  1389.6 28.1 reduce-scatter.16
  1420.0 112.8 reduce-scatter.26
  1535.2 52.5 all-reduce.3
  1590.1 112.8 reduce-scatter.30
where the time goes:
time: 1780 us; the launch traced here: 1770 us
  waiting for transfers between devices  919 us (52%)
  matrix products  495 us (28%)
  local copies, waits for them, and re-layouts  199 us (11%)
  other arithmetic  89.5 us (5%)
  blocking collectives  52.7 us (3%)
    unnamed x20, waiting for transfers between devices  419 us
    dot_general x4, matrix products, one_part(): jnp.einsum('hbl,lhe->bhe', logit_grad, key_heads, preferred_element_type=...  125 us
    all_gather x1, waiting for transfers between devices, local(): first_gathered = lax.all_gather(first_rows, 'tensor', axis=1, tiled=True)  121 us
    dot_general x4, matrix products, one_part(): jnp.einsum('hbl,bhe->lhe', logit_grad, query_part, preferred_element_type...  120 us
    all_gather x1, waiting for transfers between devices, local(): second_gathered = lax.all_gather(second_rows, 'tensor', axis=1, tiled=True)  120 us
    all_gather x1, waiting for transfers between devices, local(): feed_grad_gathered = lax.all_gather(feed_grad, 'tensor', axis=1, tiled=True)  119 us
    unnamed x117, local copies, waits for them, and re-layouts  103 us
    all_gather x1, waiting for transfers between devices, local(): branch_gathered = lax.all_gather(branch_grad, 'tensor', axis=1, tiled=True)  60.8 us
  transfers between devices with their start and end apart: 16, of which 13 were waited for; matrix products, arithmetic and copies ran while one was open for 32% of the time, Pallas kernels for 0%

commit v1 on v0

--- a/solution.py
+++ b/solution.py
@@ -277,7 +277,9 @@
         ).astype(jnp.float32),
     )
     large_sums = (
-        lax.psum(group_parts[0].astype(jnp.bfloat16), "cross").astype(jnp.float32),
+        jnp.sum(jax.lax.all_gather(group_parts[0].astype(jnp.bfloat16), "cross"), 0).astype(
+            jnp.float32
+        ),
         lax.psum(group_parts[1].astype(jnp.bfloat16), "cross").astype(jnp.float32),
         lax.psum(group_parts[2].astype(jnp.bfloat16), "cross").astype(jnp.float32),
         lax.psum(group_parts[3].astype(jnp.bfloat16), "cross").astype(jnp.float32),

time: 1780 us -> 1660 us (0.933)
  waiting for transfers between devices: 919 us -> 787 us
    unnamed x20, waiting for transfers between devices: 419 us -> 324 us
    psum x1, waiting for transfers between devices: 48.4 us -> 0.01 us  [local(): lax.psum(group_parts[1].astype(jnp.bfloat16), 'cross').astype(jnp.float32)]
    unnamed x117 -> x114, local copies, waits for them, and re-layouts: 103 us -> 104 us
  transfers between devices with their start and end apart: 16 -> 16, of which waited for: 13 -> 11; matrix products, arithmetic and copies ran while one was open for 32% -> 34% of each run, Pallas kernels for 0% -> 0%
where the time goes in v1:
time: 1660 us; the launch traced here: 1650 us
  waiting for transfers between devices  787 us (47%)
  matrix products  494 us (30%)
  local copies, waits for them, and re-layouts  201 us (12%)
  other arithmetic  90.7 us (5%)
  blocking collectives  64 us (4%)
    unnamed x20, waiting for transfers between devices  324 us
    dot_general x4, matrix products, one_part(): jnp.einsum('hbl,lhe->bhe', logit_grad, key_heads, preferred_element_type=...  125 us
    all_gather x1, waiting for transfers between devices, local(): first_gathered = lax.all_gather(first_rows, 'tensor', axis=1, tiled=True)  121 us
    dot_general x4, matrix products, one_part(): jnp.einsum('hbl,bhe->lhe', logit_grad, query_part, preferred_element_type...  120 us
    all_gather x1, waiting for transfers between devices, local(): second_gathered = lax.all_gather(second_rows, 'tensor', axis=1, tiled=True)  120 us
    all_gather x1, waiting for transfers between devices, local(): feed_grad_gathered = lax.all_gather(feed_grad, 'tensor', axis=1, tiled=True)  119 us
    unnamed x114, local copies, waits for them, and re-layouts  104 us
    all_gather x1, waiting for transfers between devices, local(): branch_gathered = lax.all_gather(branch_grad, 'tensor', axis=1, tiled=True)  60.7 us
  transfers between devices with their start and end apart: 16, of which 11 were waited for; matrix products, arithmetic and copies ran while one was open for 34% of the time, Pallas kernels for 0%

profile of v1, /device:TPU:0, one launch (start us, length us, event | category | flops | bytes accessed | tf_op | source)
XLA Modules:
  0.0 1654.8 jit_solution(4293863833872528642)
XLA Ops:
  15.8 10.8 all_gather.32
  26.7 6.8 all-gather.11.cloned.1.call-done
  33.5 120.5 %all-gather.9.cloned.1.call-done = bf16[2,1568,1024]{2,1,0:T(8,128)(2,1)} async-done(((bf16[2,392,1024]{2,1,0:T(8,128)(2,1)}), bf16[2,1568,1024]{2,1,0:T(8,128)(2,1)}) %all-gather.9.cloned.1.call-update) | async-done | bytes 6422544 | tf_op jit(solution)/shard_map/all_gather | solution.py:155
  154.0 7.8 fusion.79
  173.8 81.3 %while.54 = (s32[]{:T(128)}, bf16[2,1568,256]{1,2,0:T(8,128)(2,1)}, f32[2,2,4,784,1]{3,2,1,4,0:T(4,128)}, bf16[2,1568,256]{1,2,0:T(8,128)(2,1)}, bf16[2,1568,256...) while((s32[]{:T(128)}, bf16[2,1568,256]{1,2,0:T(8,128)(2,1)}, ...), condition=%wide.region_7.8_spmd, body=%wide.region_2.7_spmd.sunk | while | flops 1303268352 | bytes 87527496 | solution.py:166
  180.3 30.0 %while.57 = (s32[]{:T(128)}, bf16[2,784,4,64]{1,3,2,0:T(8,128)(2,1)}, f32[2,4,784,1]{2,1,3,0:T(4,128)S(1)}, bf16[2,784,4,64]{1,3,2,0:T(8,128)(2,1)}, bf16[1568,4...) while((s32[]{:T(128)}, bf16[2,784,4,64]{1,3,2,0:T(8,128)(2,1)}, ...), condition=%wide.region_6.6_spmd, body=%wide.region_3.5_spmd.sunk | while | flops 1303268352 | bytes 61734240 | solution.py:48
  188.7 6.5 fusion.183
  203.7 6.5 fusion.183
  220.8 30.0 %while.57 = (s32[]{:T(128)}, bf16[2,784,4,64]{1,3,2,0:T(8,128)(2,1)}, f32[2,4,784,1]{2,1,3,0:T(4,128)S(1)}, bf16[2,784,4,64]{1,3,2,0:T(8,128)(2,1)}, bf16[1568,4...) while((s32[]{:T(128)}, bf16[2,784,4,64]{1,3,2,0:T(8,128)(2,1)}, ...), condition=%wide.region_6.6_spmd, body=%wide.region_3.5_spmd.sunk | while | flops 1303268352 | bytes 61734240 | solution.py:48
  229.2 6.5 fusion.183
  244.2 6.5 fusion.183
  259.2 14.0 copy.84
  273.2 5.3 copy.99
  279.3 110.5 %reduce-scatter.25.cloned.1.call-done = bf16[392,2048]{1,0:T(8,128)(2,1)} async-done(((bf16[1568,2048]{1,0:T(8,128)(2,1)}), bf16[392,2048]{1,0:T(8,128)(2,1)}) %reduce-scatter.25.cloned.1.call-update) | async-done | bytes 1605648
  403.3 11.1 all-gather.15.cloned.1.call-done
  414.3 119.5 %all-gather.13.cloned.1.call-done = bf16[2,1568,1024]{2,1,0:T(8,128)(2,1)} async-done(((bf16[2,392,1024]{2,1,0:T(8,128)(2,1)}), bf16[2,1568,1024]{2,1,0:T(8,128)(2,1)}) %all-gather.13.cloned.1.call-update) | async-done | bytes 6422544 | tf_op jit(solution)/shard_map/all_gather | solution.py:186
  533.8 19.8 %fusion.109 = (u8[1568,1024]{1,0:T(8,128)(4,1)}, u8[1568,1024]{1,0:T(8,128)(4,1)}, f32[2,1568,1024]{2,1,0:T(8,128)}) fusion(f32[1024]{0:T(1024)S(1)} %convert_element_type.190, bf16[2,1568,1024]{2,1,0:T(8,128)(2,1)} %all-gather.13.cloned.1.call-done, bf16[1024,1024]{1,0:T(8,128)(2,1)} %all-gather.15.cloned.1.call-done), kind=kOutput, calls=%fused_computation.148 | convolution fusion | flops 6618415104 | bytes 24580096 | tf_op jit(solution)/shard_map/njz,zc->njc/dot_general | solution.py:187
  556.3 119.1 %all-gather.19.cloned.1.call-done = bf16[2,1568,1024]{2,1,0:T(8,128)(2,1)} async-done(((bf16[2,392,1024]{2,1,0:T(8,128)(2,1)}), bf16[2,1568,1024]{2,1,0:T(8,128)(2,1)}) %all-gather.19.cloned.1.call-update) | async-done | bytes 6422544 | tf_op jit(solution)/shard_map/all_gather | solution.py:202
  675.4 15.1 convert_reduce_fusion
  690.5 7.5 convolution_convert_fusion
  698.0 13.7 copy.88
  711.8 5.4 copy.101
  717.2 111.2 %reduce-scatter.29.cloned.1.call-done = bf16[392,2048]{1,0:T(8,128)(2,1)} async-done(((bf16[1568,2048]{1,0:T(8,128)(2,1)}), bf16[392,2048]{1,0:T(8,128)(2,1)}) %reduce-scatter.29.cloned.1.call-update) | async-done | bytes 1605648
  828.4 5.3 reshape.179
  841.8 12.6 bitcast_convert_fusion.2
  854.5 31.3 %fusion.62 = bf16[2,1568,1024]{2,1,0:T(8,128)(2,1)S(1)} fusion(f32[2,1568,1024]{2,1,0:T(8,128)} %get-tuple-element.401, f32[1024]{0:T(1024)S(1)} %convert_element_type.190, u8[1568,1024]{1,0:T(8,128)(4,1)S(1)} %copy-done.29, u8[1568,1024]{1,0:T(8,128)(4,1)S(1)} %copy-done.28), kind=kLoop, calls=%fused_computation.65 | loop fusion | flops 227999744 | bytes 22482944 | tf_op jit(solution)/shard_map/convert_element_type | solution.py:191
  888.5 10.6 bitcast_convert_fusion.1
  899.2 60.7 %all-gather.21.cloned.1.call-done = bf16[2,1568,1024]{2,1,0:T(8,128)(2,1)} async-done(((bf16[2,392,1024]{2,1,0:T(8,128)(2,1)}), bf16[2,1568,1024]{2,1,0:T(8,128)(2,1)}) %all-gather.21.cloned.1.call-update) | async-done | bytes 6422544 | tf_op jit(solution)/shard_map/all_gather | solution.py:231
  959.9 5.5 fusion.122
  965.5 11.2 convolution_convert_fusion.1
  976.7 13.7 copy.86
  990.4 5.4 copy.100
  1004.3 387.9 %while.56 = (s32[]{:T(128)}, bf16[2,1568,256]{1,2,0:T(8,128)(2,1)}, bf16[2,1568,256]{2,1,0:T(8,128)(2,1)}, bf16[2,1568,256]{1,2,0:T(8,128)(2,1)}, bf16[2,1568,25...) while((s32[]{:T(128)}, bf16[2,1568,256]{1,2,0:T(8,128)(2,1)}, ...), condition=%wide.region_19.20_spmd, body=%wide.region_15.19_spmd.sunk | while | flops 3213581312 | bytes 417577472 | solution.py:238
  1014.6 173.9 %while.58 = (s32[]{:T(128)}, f32[1568,4,64]{0,2,1:T(8,128)}, f32[1568,4,64]{0,2,1:T(8,128)}, bf16[2,784,4,64]{1,3,2,0:T(8,128)(2,1)}, bf16[2,784,4,64]{1,3,2,0:T...) while((s32[]{:T(128)}, f32[1568,4,64]{0,2,1:T(8,128)}, ...), condition=%wide.region_18.18_spmd.clone, body=%wide.region_16.17_spmd.clone.sunk | while | flops 3212778496 | bytes 332231680 | solution.py:88
  1014.6 5.1 subtract_exponential_fusion.3
  1019.7 5.1 fusion.178
  1027.4 11.4 fusion.176
  1038.8 31.2 %fusion.179 = bf16[2,784,4,64]{1,3,2,0:T(8,128)(2,1)} fusion(bf16[2,784,4,64]{1,3,2,0:T(8,128)(2,1)} %get-tuple-element.679, s32[]{:T(128)S(6)} %copy.169, bf16[1568,4,64]{0,2,1:T(8,128)(2,1)} %get-tuple-element.692, f32[4,784,1568]{2,1,0:T(8,128)} %copy-done, f32[4,784,1568]{2,1,0:T(8,128)} %fusion.176), kind=kOutput, calls=%fused_computation.34.clone.1 | convolution fusion | flops 654199424 | bytes 84803584 | tf_op jit(solution)/shard_map/while/body/eval_jaxpr/while/body/eval_jaxpr/hbl,lhe->bhe/dot_general | solution.py:73
  1070.0 30.1 %fusion.177 = f32[1568,4,64]{0,2,1:T(8,128)S(1)} fusion(f32[4,784,1568]{2,1,0:T(8,128)} %copy-done, f32[4,784,1568]{2,1,0:T(8,128)} %fusion.176, f32[1568,4,64]{0,2,1:T(8,128)S(1)} %copy-done.13, pred[]{:T(512)S(6)} %compare.3, bf16[2,784,4,64]{1,3,2,0:T(8,128)(2,1)S(1)} %copy-done.2, s32[]{:T(128)S(6)} %copy.169), kind=kOutput, calls=%fused_computation.30.clone.1 | convolution fusion | flops 654801536 | bytes 87261192 | tf_op jit(solution)/shard_map/while/body/eval_jaxpr/while/body/eval_jaxpr/hbl,bhe->lhe/dot_general | solution.py:76
  1106.4 7.1 fusion.178
  1114.8 11.2 fusion.176
  1126.0 31.2 %fusion.179 = bf16[2,784,4,64]{1,3,2,0:T(8,128)(2,1)} fusion(bf16[2,784,4,64]{1,3,2,0:T(8,128)(2,1)} %get-tuple-element.679, s32[]{:T(128)S(6)} %copy.169, bf16[1568,4,64]{0,2,1:T(8,128)(2,1)} %get-tuple-element.692, f32[4,784,1568]{2,1,0:T(8,128)} %copy-done, f32[4,784,1568]{2,1,0:T(8,128)} %fusion.176), kind=kOutput, calls=%fused_computation.34.clone.1 | convolution fusion | flops 654199424 | bytes 84803584 | tf_op jit(solution)/shard_map/while/body/eval_jaxpr/while/body/eval_jaxpr/hbl,lhe->bhe/dot_general | solution.py:73
  1157.2 30.1 %fusion.177 = f32[1568,4,64]{0,2,1:T(8,128)S(1)} fusion(f32[4,784,1568]{2,1,0:T(8,128)} %copy-done, f32[4,784,1568]{2,1,0:T(8,128)} %fusion.176, f32[1568,4,64]{0,2,1:T(8,128)S(1)} %copy-done.13, pred[]{:T(512)S(6)} %compare.3, bf16[2,784,4,64]{1,3,2,0:T(8,128)(2,1)S(1)} %copy-done.2, s32[]{:T(128)S(6)} %copy.169), kind=kOutput, calls=%fused_computation.30.clone.1 | convolution fusion | flops 654801536 | bytes 87261192 | tf_op jit(solution)/shard_map/while/body/eval_jaxpr/while/body/eval_jaxpr/hbl,bhe->lhe/dot_general | solution.py:76
  1208.7 173.3 %while.58 = (s32[]{:T(128)}, f32[1568,4,64]{0,2,1:T(8,128)}, f32[1568,4,64]{0,2,1:T(8,128)}, bf16[2,784,4,64]{1,3,2,0:T(8,128)(2,1)}, bf16[2,784,4,64]{1,3,2,0:T...) while((s32[]{:T(128)}, f32[1568,4,64]{0,2,1:T(8,128)}, ...), condition=%wide.region_18.18_spmd.clone, body=%wide.region_16.17_spmd.clone.sunk | while | flops 3212778496 | bytes 332231680 | solution.py:88
  1208.7 5.1 subtract_exponential_fusion.3
  1213.8 5.1 fusion.178
  1221.3 11.2 fusion.176
  1232.5 31.2 %fusion.179 = bf16[2,784,4,64]{1,3,2,0:T(8,128)(2,1)} fusion(bf16[2,784,4,64]{1,3,2,0:T(8,128)(2,1)} %get-tuple-element.679, s32[]{:T(128)S(6)} %copy.169, bf16[1568,4,64]{0,2,1:T(8,128)(2,1)} %get-tuple-element.692, f32[4,784,1568]{2,1,0:T(8,128)} %copy-done, f32[4,784,1568]{2,1,0:T(8,128)} %fusion.176), kind=kOutput, calls=%fused_computation.34.clone.1 | convolution fusion | flops 654199424 | bytes 84803584 | tf_op jit(solution)/shard_map/while/body/eval_jaxpr/while/body/eval_jaxpr/hbl,lhe->bhe/dot_general | solution.py:73
  1263.7 30.1 %fusion.177 = f32[1568,4,64]{0,2,1:T(8,128)S(1)} fusion(f32[4,784,1568]{2,1,0:T(8,128)} %copy-done, f32[4,784,1568]{2,1,0:T(8,128)} %fusion.176, f32[1568,4,64]{0,2,1:T(8,128)S(1)} %copy-done.13, pred[]{:T(512)S(6)} %compare.3, bf16[2,784,4,64]{1,3,2,0:T(8,128)(2,1)S(1)} %copy-done.2, s32[]{:T(128)S(6)} %copy.169), kind=kOutput, calls=%fused_computation.30.clone.1 | convolution fusion | flops 654801536 | bytes 87261192 | tf_op jit(solution)/shard_map/while/body/eval_jaxpr/while/body/eval_jaxpr/hbl,bhe->lhe/dot_general | solution.py:76
  1300.1 7.1 fusion.178
  1308.3 11.2 fusion.176
  1319.5 31.2 %fusion.179 = bf16[2,784,4,64]{1,3,2,0:T(8,128)(2,1)} fusion(bf16[2,784,4,64]{1,3,2,0:T(8,128)(2,1)} %get-tuple-element.679, s32[]{:T(128)S(6)} %copy.169, bf16[1568,4,64]{0,2,1:T(8,128)(2,1)} %get-tuple-element.692, f32[4,784,1568]{2,1,0:T(8,128)} %copy-done, f32[4,784,1568]{2,1,0:T(8,128)} %fusion.176), kind=kOutput, calls=%fused_computation.34.clone.1 | convolution fusion | flops 654199424 | bytes 84803584 | tf_op jit(solution)/shard_map/while/body/eval_jaxpr/while/body/eval_jaxpr/hbl,lhe->bhe/dot_general | solution.py:73
  1350.6 30.1 %fusion.177 = f32[1568,4,64]{0,2,1:T(8,128)S(1)} fusion(f32[4,784,1568]{2,1,0:T(8,128)} %copy-done, f32[4,784,1568]{2,1,0:T(8,128)} %fusion.176, f32[1568,4,64]{0,2,1:T(8,128)S(1)} %copy-done.13, pred[]{:T(512)S(6)} %compare.3, bf16[2,784,4,64]{1,3,2,0:T(8,128)(2,1)S(1)} %copy-done.2, s32[]{:T(128)S(6)} %copy.169), kind=kOutput, calls=%fused_computation.30.clone.1 | convolution fusion | flops 654801536 | bytes 87261192 | tf_op jit(solution)/shard_map/while/body/eval_jaxpr/while/body/eval_jaxpr/hbl,bhe->lhe/dot_general | solution.py:76
  1397.4 9.9 fusion.119
  1407.4 7.4 bitcast_convert_fusion
  1414.8 13.7 copy.90
  1428.5 5.3 copy.102
  1434.8 5.4 reshape.177
  1447.2 22.3 %reduce-scatter.17.cloned.1.call-done = bf16[3,256,256]{1,2,0:T(8,128)(2,1)} async-done(((bf16[3,1024,256]{1,2,0:T(8,128)(2,1)}), bf16[3,256,256]{1,2,0:T(8,128)(2,1)}) %reduce-scatter.17.cloned.1.call-update) | async-done | bytes 393232 | tf_op jit(solution)/shard_map/reduce_scatter | solution.py:266
  1470.7 11.5 all-gather
  1483.9 100.8 %reduce-scatter.31.cloned.1.call-done = bf16[392,2048]{1,0:T(8,128)(2,1)} async-done(((bf16[1568,2048]{1,0:T(8,128)(2,1)}), bf16[392,2048]{1,0:T(8,128)(2,1)}) %reduce-scatter.31.cloned.1.call-update) | async-done | bytes 1605648
  1584.7 5.6 reshape.181
  1593.5 41.6 %all-reduce = (f32[1024]{0:T(1024)S(1)}, f32[1024]{0:T(1024)S(1)}, f32[1024]{0:T(1024)S(1)}, f32[1024]{0:T(1024)S(1)}, f32[1024]{0:T(1024)S(1)}, /*index=5*/f32[...) all-reduce(f32[1024]{0:T(1024)S(1)} %get-tuple-element.308, ...), channel_id=1, replica_groups=mesh['tensor'=4,'group'=4,'cross'=2] {'tensor','group','cross'}, use_global_device_ids=true, to_apply=%region_24.25 | all-reduce | flops 12288 | bytes 98304 | tf_op jit(solution)/shard_map/psum | solution.py:287
  1640.8 7.1 fusion.97
  (357 shorter events, 202.1 us)
Async XLA Ops:
  7.2 6.6 copy-start.3
  7.2 26.3 %all-gather.11.cloned.1.call-start = ((), (), s32[]{:S(2)}) async-start(), calls=%async_computation.9 | async-start | bytes 1966080 | tf_op jit(solution)/shard_map/all_gather | solution.py:145
  7.9 146.1 %all-gather.9.cloned.1.call-start = ((), (), s32[]{:S(2)}) async-start(), calls=%async_computation.8 | async-start | bytes 8028160 | tf_op jit(solution)/shard_map/all_gather | solution.py:155
  15.6 374.2 %reduce-scatter.25.cloned.1.call-start = ((), (), s32[]{:S(2)}) async-start(), calls=%async_computation.19 | async-start | bytes 8028160
  174.0 6.3 copy-start.8
  214.6 6.2 copy-start.8
  278.5 115.7 %copy-start.4 = (bf16[2,392,1024]{2,1,0:T(8,128)(2,1)S(1)}, bf16[2,392,1024]{2,1,0:T(8,128)(2,1)}, u32[]{:S(2)}) copy-start(bf16[2,392,1024]{2,1,0:T(8,128)(2,1)} %param.24) | copy-start | bytes 4816900
  278.6 135.8 %all-gather.15.cloned.1.call-start = ((), (), s32[]{:S(2)}) async-start(), calls=%async_computation.11 | async-start | bytes 2621440 | tf_op jit(solution)/shard_map/all_gather | solution.py:147
  279.1 254.7 %all-gather.13.cloned.1.call-start = ((), (), s32[]{:S(2)}) async-start(), calls=%async_computation.10 | async-start | bytes 8028160 | tf_op jit(solution)/shard_map/all_gather | solution.py:186
  279.2 558.7 %copy-start.30 = (f32[1024]{0:T(1024)}, f32[1024]{0:T(1024)S(1)}, u32[]{:S(2)}) copy-start(f32[1024]{0:T(1024)S(1)} %convert_element_type.186) | copy-start | bytes 12292
  279.2 558.7 %copy-start.37 = (f32[1024]{0:T(1024)}, f32[1024]{0:T(1024)S(1)}, u32[]{:S(2)}) copy-start(f32[1024]{0:T(1024)S(1)} %convert_element_type.187) | copy-start | bytes 12292
  394.3 443.7 %copy-start.6 = (bf16[392,2,1024]{2,1,0:T(2,128)(2,1)}, bf16[392,2,1024]{2,1,0:T(2,128)(2,1)S(1)}, u32[]{:S(2)}) copy-start(bf16[392,2,1024]{2,1,0:T(2,128)(2,1)S(1)} %reshape.175) | copy-start | bytes 4816900
  394.9 443.1 %copy-start.32 = (f32[2,392]{1,0:T(2,128)}, f32[2,392]{1,0:T(2,128)S(1)}, u32[]{:S(2)}) copy-start(f32[2,392]{1,0:T(2,128)S(1)} %broadcast_multiply_fusion.4) | copy-start | bytes 9412
  395.8 442.2 %copy-start.39 = (f32[2,392]{1,0:T(2,128)}, f32[2,392]{1,0:T(2,128)S(1)}, u32[]{:S(2)}) copy-start(f32[2,392]{1,0:T(2,128)S(1)} %add_rsqrt_fusion) | copy-start | bytes 9412
  397.8 5.4 copy-start.59
  397.8 158.5 %all-gather.17.cloned.1.call-start = ((), (), s32[]{:S(2)}) async-start(), calls=%async_computation.12 | async-start | bytes 2621440 | tf_op jit(solution)/shard_map/all_gather | solution.py:148
  398.4 277.0 %all-gather.19.cloned.1.call-start = ((), (), s32[]{:S(2)}) async-start(), calls=%async_computation.13 | async-start | bytes 8028160 | tf_op jit(solution)/shard_map/all_gather | solution.py:202
  399.1 438.9 %copy-start.53 = (f32[2]{0:T(128)}, f32[2]{0:T(128)S(1)}, u32[]{:S(2)}) copy-start(f32[2]{0:T(128)S(1)} %compare_convert_fusion) | copy-start | bytes 28
  403.2 425.2 %reduce-scatter.29.cloned.1.call-start = ((), (), s32[]{:S(2)}) async-start(), calls=%async_computation.21 | async-start | bytes 8028160
  675.4 15.1 copy-start.61
  690.5 7.5 copy-start.64
  717.2 242.7 %all-gather.21.cloned.1.call-start = ((), (), s32[]{:S(2)}) async-start(), calls=%async_computation.14 | async-start | bytes 8028160 | tf_op jit(solution)/shard_map/all_gather | solution.py:231
  841.7 12.8 copy-start.28
  841.7 12.8 copy-start.29
  841.8 555.5 %reduce-scatter.21.cloned.1.call-start = ((), (), s32[]{:S(2)}) async-start(), calls=%async_computation.17 | async-start | bytes 2621440 | tf_op jit(solution)/shard_map/reduce_scatter | solution.py:272
  854.5 542.8 %reduce-scatter.23.cloned.1.call-start = ((), (), s32[]{:S(2)}) async-start(), calls=%async_computation.18 | async-start | bytes 2621440 | tf_op jit(solution)/shard_map/reduce_scatter | solution.py:275
  888.5 71.4 %copy-start.25 = (bf16[2,1568,256]{1,2,0:T(8,128)(2,1)S(1)}, bf16[2,1568,256]{1,2,0:T(8,128)(2,1)}, u32[]{:S(2)}) copy-start(bf16[2,1568,256]{1,2,0:T(8,128)(2,1)} %get-tuple-element.179) | copy-start | bytes 4816900
  899.1 498.1 %reduce-scatter.19.cloned.1.call-start = ((), (), s32[]{:S(2)}) async-start(), calls=%async_computation.16 | async-start | bytes 655360 | tf_op jit(solution)/shard_map/reduce_scatter | solution.py:269
  965.5 469.4 %reduce-scatter.27.cloned.1.call-start = ((), (), s32[]{:S(2)}) async-start(), calls=%async_computation.20 | async-start | bytes 8028160
  995.9 445.5 %all-reduce.4.cloned.1.call-start = ((), (), s32[]{:S(2)}) async-start(), calls=%async_computation.23 | async-start | bytes 2359296 | tf_op jit(solution)/shard_map/psum | solution.py:283
  1006.3 5.2 copy-start.11
  1019.7 7.7 copy-start
  1038.8 31.2 %copy-start.2 = (bf16[2,784,4,64]{1,3,2,0:T(8,128)(2,1)S(1)}, bf16[2,784,4,64]{1,3,2,0:T(8,128)(2,1)}, u32[]{:S(2)}) copy-start(bf16[2,784,4,64]{1,3,2,0:T(8,128)(2,1)} %get-tuple-element.691) | copy-start | bytes 2408452 | tf_op jit(solution)/shard_map/while/body/eval_jaxpr/while
  1038.8 31.2 %copy-start.13 = (f32[1568,4,64]{0,2,1:T(8,128)S(1)}, f32[1568,4,64]{0,2,1:T(8,128)}, u32[]{:S(2)}) copy-start(f32[1568,4,64]{0,2,1:T(8,128)} %get-tuple-element.677) | copy-start | bytes 4816900 | tf_op jit(solution)/shard_map/while/body/eval_jaxpr/while
  1106.4 8.3 copy-start
  1126.0 31.2 %copy-start.2 = (bf16[2,784,4,64]{1,3,2,0:T(8,128)(2,1)S(1)}, bf16[2,784,4,64]{1,3,2,0:T(8,128)(2,1)}, u32[]{:S(2)}) copy-start(bf16[2,784,4,64]{1,3,2,0:T(8,128)(2,1)} %get-tuple-element.691) | copy-start | bytes 2408452 | tf_op jit(solution)/shard_map/while/body/eval_jaxpr/while
  1126.0 31.2 %copy-start.13 = (f32[1568,4,64]{0,2,1:T(8,128)S(1)}, f32[1568,4,64]{0,2,1:T(8,128)}, u32[]{:S(2)}) copy-start(f32[1568,4,64]{0,2,1:T(8,128)} %get-tuple-element.677) | copy-start | bytes 4816900 | tf_op jit(solution)/shard_map/while/body/eval_jaxpr/while
  1191.2 5.1 copy-start.1
  1200.4 5.2 copy-start.11
  1213.8 7.6 copy-start
  1232.5 31.2 %copy-start.2 = (bf16[2,784,4,64]{1,3,2,0:T(8,128)(2,1)S(1)}, bf16[2,784,4,64]{1,3,2,0:T(8,128)(2,1)}, u32[]{:S(2)}) copy-start(bf16[2,784,4,64]{1,3,2,0:T(8,128)(2,1)} %get-tuple-element.691) | copy-start | bytes 2408452 | tf_op jit(solution)/shard_map/while/body/eval_jaxpr/while
  1232.5 31.2 %copy-start.13 = (f32[1568,4,64]{0,2,1:T(8,128)S(1)}, f32[1568,4,64]{0,2,1:T(8,128)}, u32[]{:S(2)}) copy-start(f32[1568,4,64]{0,2,1:T(8,128)} %get-tuple-element.677) | copy-start | bytes 4816900 | tf_op jit(solution)/shard_map/while/body/eval_jaxpr/while
  1300.1 8.2 copy-start
  1319.5 31.2 %copy-start.2 = (bf16[2,784,4,64]{1,3,2,0:T(8,128)(2,1)S(1)}, bf16[2,784,4,64]{1,3,2,0:T(8,128)(2,1)}, u32[]{:S(2)}) copy-start(bf16[2,784,4,64]{1,3,2,0:T(8,128)(2,1)} %get-tuple-element.691) | copy-start | bytes 2408452 | tf_op jit(solution)/shard_map/while/body/eval_jaxpr/while
  1319.5 31.2 %copy-start.13 = (f32[1568,4,64]{0,2,1:T(8,128)S(1)}, f32[1568,4,64]{0,2,1:T(8,128)}, u32[]{:S(2)}) copy-start(f32[1568,4,64]{0,2,1:T(8,128)} %get-tuple-element.677) | copy-start | bytes 4816900 | tf_op jit(solution)/shard_map/while/body/eval_jaxpr/while
  1397.3 72.2 %reduce-scatter.17.cloned.1.call-start = ((), (), s32[]{:S(2)}) async-start(), calls=%async_computation.15 | async-start | bytes 1966080 | tf_op jit(solution)/shard_map/reduce_scatter | solution.py:266
  1407.3 177.3 %reduce-scatter.31.cloned.1.call-start = ((), (), s32[]{:S(2)}) async-start(), calls=%async_computation.22 | async-start | bytes 8028160
  1433.9 6.3 copy-start.18
  1482.2 108.0 %copy-start.5 = (bf16[2,392,1024]{2,1,0:T(8,128)(2,1)S(1)}, bf16[2,392,1024]{2,1,0:T(8,128)(2,1)}, u32[]{:S(2)}) copy-start(bf16[2,392,1024]{2,1,0:T(8,128)(2,1)} %param.24) | copy-start | bytes 4816900
  1482.2 108.0 %copy-start.36 = (f32[2,392]{1,0:T(2,128)S(1)}, f32[2,392]{1,0:T(2,128)}, u32[]{:S(2)}) copy-start(f32[2,392]{1,0:T(2,128)} %copy-done.35) | copy-start | bytes 9412
  1482.2 108.0 %copy-start.42 = (f32[1024]{0:T(1024)S(1)}, f32[1024]{0:T(1024)}, u32[]{:S(2)}) copy-start(f32[1024]{0:T(1024)} %copy-done.41) | copy-start | bytes 12292
  1482.2 108.0 %copy-start.44 = (f32[2,392]{1,0:T(2,128)S(1)}, f32[2,392]{1,0:T(2,128)}, u32[]{:S(2)}) copy-start(f32[2,392]{1,0:T(2,128)} %copy-done.43) | copy-start | bytes 9412
  1483.8 109.7 %copy-start.49 = (f32[1024]{0:T(1024)S(1)}, f32[1024]{0:T(1024)}, u32[]{:S(2)}) copy-start(f32[1024]{0:T(1024)} %get-tuple-element.386) | copy-start | bytes 12292
  1483.8 109.7 %copy-start.50 = (f32[1024]{0:T(1024)S(1)}, f32[1024]{0:T(1024)}, u32[]{:S(2)}) copy-start(f32[1024]{0:T(1024)} %get-tuple-element.306) | copy-start | bytes 12292
  1483.8 109.7 %copy-start.51 = (f32[1024]{0:T(1024)S(1)}, f32[1024]{0:T(1024)}, u32[]{:S(2)}) copy-start(f32[1024]{0:T(1024)} %get-tuple-element.312) | copy-start | bytes 12292
  1483.8 109.7 %copy-start.52 = (f32[1024]{0:T(1024)S(1)}, f32[1024]{0:T(1024)}, u32[]{:S(2)}) copy-start(f32[1024]{0:T(1024)} %get-tuple-element.388) | copy-start | bytes 12292
  1483.8 156.9 %copy-start.7 = (bf16[392,2,1024]{2,1,0:T(2,128)(2,1)S(1)}, bf16[392,2,1024]{2,1,0:T(2,128)(2,1)}, u32[]{:S(2)}) copy-start(bf16[392,2,1024]{2,1,0:T(2,128)(2,1)} %copy-done.6) | copy-start | bytes 4816900
  1483.8 156.9 %copy-start.31 = (f32[1024]{0:T(1024)S(1)}, f32[1024]{0:T(1024)}, u32[]{:S(2)}) copy-start(f32[1024]{0:T(1024)} %copy-done.30) | copy-start | bytes 12292
  1483.8 156.9 %copy-start.33 = (f32[2,392]{1,0:T(2,128)S(1)}, f32[2,392]{1,0:T(2,128)}, u32[]{:S(2)}) copy-start(f32[2,392]{1,0:T(2,128)} %copy-done.32) | copy-start | bytes 9412
  1483.8 156.9 %copy-start.38 = (f32[1024]{0:T(1024)S(1)}, f32[1024]{0:T(1024)}, u32[]{:S(2)}) copy-start(f32[1024]{0:T(1024)} %copy-done.37) | copy-start | bytes 12292
  1483.8 156.9 %copy-start.40 = (f32[2,392]{1,0:T(2,128)S(1)}, f32[2,392]{1,0:T(2,128)}, u32[]{:S(2)}) copy-start(f32[2,392]{1,0:T(2,128)} %copy-done.39) | copy-start | bytes 9412
  1483.8 156.9 %copy-start.46 = (f32[2,392]{1,0:T(2,128)S(1)}, f32[2,392]{1,0:T(2,128)}, u32[]{:S(2)}) copy-start(f32[2,392]{1,0:T(2,128)} %copy-done.45) | copy-start | bytes 9412
  1483.9 156.9 %copy-start.48 = (f32[2,392]{1,0:T(2,128)S(1)}, f32[2,392]{1,0:T(2,128)}, u32[]{:S(2)}) copy-start(f32[2,392]{1,0:T(2,128)} %copy-done.47) | copy-start | bytes 9412
  1483.9 156.9 %copy-start.54 = (f32[2]{0:T(128)S(1)}, f32[2]{0:T(128)}, u32[]{:S(2)}) copy-start(f32[2]{0:T(128)} %copy-done.53) | copy-start | bytes 28
  (40 other events, 98.3 us)
Sparse Core Ops, SparseCore 0:
  9.6 23.8 all-gather.10
  35.6 118.3 all-gather.8
  278.7 111.0 reduce-scatter.24
  391.2 23.0 all-gather.14
  416.3 117.4 all-gather.12
  535.2 21.0 all-gather.16
  557.9 117.4 all-gather.18
  717.3 111.0 reduce-scatter.28
  841.9 118.0 all-gather.20
  962.3 29.6 reduce-scatter.20
  994.6 31.4 reduce-scatter.22
  1029.0 21.6 reduce-scatter.18
  1053.1 112.8 reduce-scatter.26
  1397.4 41.3 all-reduce.3
  1441.2 28.1 reduce-scatter.16
  1471.8 112.8 reduce-scatter.30
